TPU v7x, 32 devices: a whole 2x2x4 slice. The times are simulated.
32 devices in a mesh: tm: 4 (over x, core), row: 8 (over z, y).
Axes of the slice: x: 2, y: 2, z: 4, core: 2. Of those that a mesh axis runs over, the one named last changes fastest.
Arguments:
- image: float32 [4, 1, 512, 2048], P('tm', None, 'row'), may hold values from -6 to 6
- relaxed: float32 [4, 1, 512, 2048], P('tm', None, 'row'), may hold values from -6 to 6
- dual: float32 [4, 1, 512, 2048], P('tm', None, 'row'), may hold values from -2 to 2
- sinogram: float32 [4, 12, 1, 2048], P('tm'), may hold values from -48 to 48
- angle_index: int32 [4, 12], P('tm'), may hold values from 0 to 31, as said below
- bin_offset: int32 [32, 32], P('row'), may hold values from 0 to 2047
- row_weight: float32 [32, 16], replicated, may hold values from 0.5 to 1.5
- response: bfloat16 [32, 128, 128], replicated, may hold values from -0.5 to 0.5
- row_gain: float32 [512], P('row'), may hold values from 0.6 to 11.2
Outputs:
- image_new: float32 [4, 1, 512, 2048], P('tm', None, 'row')
- dual_new: float32 [4, 1, 512, 2048], P('tm', None, 'row')
Inputs may be any that keep to these rules, and one draw needn't show every extreme that they name: `angle_index`: the 12 views of one phase name distinct entries of the angle table.
All inputs are finite; a program needn't handle non-finite values.
Results may differ from a plain program's by a relative error of at most 0.0003.
Values sent between devices are 32-bit elements; how exact they have to be, the bound alone decides.
No kernel may reach another device: no remote copies, remote signals or barrier semaphores. Data moves between devices by JAX's collectives and lax.ppermute only.
A program may use at most 64 MiB of HBM per device.

v0:
```python
import functools

import jax
import jax.numpy as jnp
from jax import lax
from jax.experimental import pallas as pl
from jax.experimental.pallas import tpu as pltpu
from jax.sharding import PartitionSpec as P


CG_ITERS = 3
TAU_STEP = 0.1
SIGMA_STEP = 2.0
LAMBDA_BOUND = 2.0
HIGH = lax.Precision.HIGHEST
LANES = 128


def halves(x):
    high = x.astype(jnp.bfloat16)
    low = (x - high.astype(jnp.float32)).astype(jnp.bfloat16)
    return high, low


def product(a, b):
    (ah, al), (bh, bl) = halves(a), halves(b)
    dot = functools.partial(jnp.dot, preferred_element_type=jnp.float32)
    return dot(ah, bh) + (dot(ah, bl) + dot(al, bh))


def lane_index(rows):
    return lax.broadcasted_iota(jnp.int32, (rows, LANES), 1)


def pull(load, offset, lane):
    block, rest = offset >> 7, offset & (LANES - 1)
    mixed = jnp.where(lane < rest, load(block + 1), load(block))
    return pltpu.roll(mixed, (LANES - rest) & (LANES - 1), 1)


def push(load, offset, lane, blocks):
    block, rest = offset >> 7, offset & (LANES - 1)
    mixed = jnp.where(lane >= LANES - rest, load(blocks - 1 - block), load(blocks - block))
    return pltpu.roll(mixed, rest, 1)


def project_sets(stack, bins, tables, zs, hd, tiles, views, blocks):
    lane = lane_index(blocks)
    rows = tiles * blocks
    total = stack.shape[0]
    for b in range(blocks):
        zs[pl.ds(b, total, stride=blocks), :] = stack[:, b * LANES : (b + 1) * LANES]
    for s, (response, angles, out, init) in enumerate(tables):
        for v in range(views):
            at = (s * views + v) * rows
            lhs = jnp.concatenate(halves(zs[at : at + rows, :]), axis=1)
            h = jnp.dot(lhs, response[v], preferred_element_type=jnp.float32)
            for k in range(tiles):
                part = h[k * blocks : (k + 1) * blocks, :]
                hd[2 * at + 2 * k * blocks : 2 * at + (2 * k + 1) * blocks, :] = part
                hd[2 * at + (2 * k + 1) * blocks : 2 * at + (2 * k + 2) * blocks, :] = part
            whole = None if init is None else init[v * blocks : (v + 1) * blocks, :]
            for k in range(tiles):
                part = push(
                    lambda q: hd[pl.ds(2 * at + 2 * k * blocks + q, blocks), :],
                    bins[k, angles[0, v]], lane, blocks,
                )
                whole = part if whole is None else whole + part
            out[v * blocks : (v + 1) * blocks, :] = whole


def project_scratch(sets, tiles, views, blocks):
    rows = sets * views * tiles * blocks
    return [pltpu.VMEM((rows, LANES), jnp.float32), pltpu.VMEM((2 * rows, LANES), jnp.float32)]


def fetch_responses(angles, response, resp, sems, views):
    copies = [
        pltpu.make_async_copy(
            response.at[angles[0, v]], resp.at[v, n * LANES : (n + 1) * LANES, :],
            sems.at[2 * v + n],
        )
        for v in range(views)
        for n in range(2)
    ]
    for copy in copies:
        copy.start()
    return copies


def view_weights(angles, gained, spread, tiles, views):
    width = gained.shape[1]
    row = lax.broadcasted_iota(jnp.int32, (tiles, width), 0)
    column = lax.broadcasted_iota(jnp.int32, (tiles, width), 1) // (width // tiles)
    for v in range(views):
        line = jnp.broadcast_to(gained[pl.ds(angles[0, v], 1), :], (tiles, width))
        spread[v * tiles : (v + 1) * tiles, :] = jnp.where(row == column, line, 0.0)


def own_kernel(
    angles, bins, weights, gain, image, dual, relaxed, response,
    resp, resp_t, spread, spread_t, table, before, rest, gained, zs, hd, chosen, table_w, table_g,
    planes, sems,
    *, tiles, views, blocks,
):
    copies = fetch_responses(angles, response, resp, sems, views)
    for n, source in enumerate((image, dual, relaxed)):
        copies.append(pltpu.make_async_copy(source, planes.at[n], sems.at[2 * views + n]))
        copies[-1].start()
    small = [
        pltpu.make_async_copy(source, target, sems.at[2 * views + 3 + n])
        for n, (source, target) in enumerate(((weights, table_w), (gain, table_g)))
    ]
    for copy in small:
        copy.start()
    for copy in small:
        copy.wait()
    width = table_w.shape[0]
    for k in range(tiles):
        gained[:, k * width : (k + 1) * width] = table_w[...].T
    gained[...] = gained[...] * table_g[...]
    view_weights(angles, gained, spread, tiles, views)
    mine = spread[...]
    spread_t[...] = mine.T
    chosen[...] = jnp.zeros_like(chosen)
    for v in range(views):
        chosen[v : v + 1, :] = gained[pl.ds(angles[0, v], 1), :]
    coupling = lax.dot_general(
        chosen[...], mine, (((1,), (1,)), ((), ())),
        precision=HIGH, preferred_element_type=jnp.float32,
    )
    table[...] = jnp.zeros_like(table)
    half = views // 2
    table[:half, : views * tiles] = coupling[:half, :]
    table[:half, LANES // 2 : LANES // 2 + views * tiles] = coupling[half:views, :]
    lane = lane_index(8)
    offsets = jnp.zeros((8, LANES), jnp.int32)
    for v in range(views):
        for k in range(tiles):
            offsets = jnp.where(lane == v * tiles + k, bins[k, angles[0, v]], offsets)
    table[half : half + 1, :] = offsets[:1, :].astype(jnp.float32)
    for copy in copies[: 2 * views + 1]:
        copy.wait()
    for v in range(views):
        turned = resp[v, :LANES, :].astype(jnp.float32).T.astype(jnp.bfloat16)
        resp_t[v, :LANES, :] = turned
        resp_t[v, LANES:, :] = turned
    project_sets(
        product(mine, planes[0]), bins, [(resp, angles, before, None)],
        zs, hd, tiles, views, blocks,
    )
    for copy in copies[2 * views + 1 :]:
        copy.wait()
    rest[...] = planes[1] - SIGMA_STEP * planes[2]


def next_kernel(angles, gained, response, resp, spread, sems, *, tiles, views):
    copies = fetch_responses(angles, response, resp, sems, views)
    view_weights(angles, gained, spread, tiles, views)
    for copy in copies:
        copy.wait()


def dual_kernel(
    angles, angles_next, bins, rest, ahead, spread, spread_next, resp, resp_next,
    before, table, dual_new, msg_own, msg_next, zs, hd, *, tiles, views, blocks,
):
    fresh = jnp.clip(rest[...] + SIGMA_STEP * ahead[...], -LAMBDA_BOUND, LAMBDA_BOUND)
    dual_new[...] = fresh
    both = jnp.concatenate([TAU_STEP * spread[...], -TAU_STEP * spread_next[...]], axis=0)
    project_sets(
        product(both, fresh), bins,
        [(resp, angles, msg_own, before), (resp_next, angles_next, msg_next, None)],
        zs, hd, tiles, views, blocks,
    )
    msg_own[views * blocks :, :] = table[...]


def couple_kernel(first, out, xs, *, size, tiles, views, blocks, table_rows):
    here = jnp.concatenate(halves(first[size:, :]), axis=0)
    count = here.shape[0]
    half_views = views // 2
    row = lax.broadcasted_iota(jnp.int32, (LANES, 2 * LANES), 0)
    column = lax.broadcasted_iota(jnp.int32, (LANES, 2 * LANES), 1)
    for k in range(tiles):
        for side in range(2):
            source = side * (LANES // 2) + (column // blocks) * tiles + k
            pick = jnp.where((row == source) & (column < views * blocks), 1.0, 0.0)
            at = (k * 2 + side) * count
            xs[at : at + count, :] = jnp.dot(
                here, pick.astype(jnp.bfloat16), preferred_element_type=jnp.float32
            )
    diagonal = (
        lax.broadcasted_iota(jnp.int32, (blocks, 2 * LANES), 1) % blocks
        == lax.broadcasted_iota(jnp.int32, (blocks, 2 * LANES), 0)
    )

    def one(device, carry):
        for k in range(tiles):
            for w in range(views):
                for piece in range(2):
                    at = (k * 2 + w // half_views) * count + piece * (count // 2) + w % half_views
                    line = xs[pl.ds(at + device * table_rows, 1), :]
                    block = jnp.where(diagonal, jnp.broadcast_to(line, diagonal.shape), 0.0)
                    rows = slice(w * blocks, (w + 1) * blocks)
                    out[device * tiles + k, piece, rows, :] = block.astype(jnp.bfloat16)
        return carry

    lax.fori_loop(0, count // (2 * table_rows), one, 0)


def cg_kernel(
    angles, bins, couple, first, second, meas, resp, resp_t, spread, image, dual_new, behind,
    out, y, d, gd, gy, step, wd, f, right, z2, zs, hd0, hd1, hd2, hd3, fs, coef, shifts_v, shifts,
    sem,
    *, tiles, views, blocks, devices, group, table_rows,
):
    hds = (hd0, hd1, hd2, hd3)
    lane = lane_index(blocks)
    size = views * blocks
    half = devices // 2
    per_device = tiles * views
    half_views = views // 2
    for n, src in enumerate((first, second)):
        there = src[pl.ds(size + half_views, half, stride=table_rows), :].astype(jnp.int32)
        back = (blocks * LANES - there) & (blocks * LANES - 1)
        for m, value in enumerate((there >> 7, there & (LANES - 1), back >> 7, back & (LANES - 1))):
            shifts_v[m * devices + n * half : m * devices + (n + 1) * half, :] = value
    to_scalars = pltpu.make_async_copy(shifts_v, shifts, sem)
    to_scalars.start()

    def turn(src, base, device, at, sign):
        mine, other = (0, 2 * devices) if sign > 0 else (2 * devices, 0)
        block = shifts[mine + device, at]
        rest = shifts[mine + devices + device, at]
        back = shifts[other + devices + device, at]
        row = base + block
        mixed = jnp.where(
            lane < rest, src[pl.ds(row + 1, blocks), :], src[pl.ds(row, blocks), :]
        )
        return pltpu.roll(mixed, back, 1)

    def double(src):
        for v in range(views):
            whole = src[v * blocks : (v + 1) * blocks, :]
            wd[2 * v * blocks : (2 * v + 1) * blocks, :] = whole
            wd[(2 * v + 1) * blocks : (2 * v + 2) * blocks, :] = whole

    def stacked(values):
        return jnp.concatenate([jnp.concatenate(halves(x), axis=1) for x in values], axis=0)

    span = group * tiles * blocks
    groups = half // group
    half_rows = half * tiles * blocks
    members = [(m, k) for m in range(group) for k in range(tiles)]

    def turned(n, g, v):
        return [
            turn(wd, 2 * v * blocks, n * half + g * group + m, v * tiles + k, 1)
            for m, k in members
        ]

    def keep_first(g, v, h):
        high, low = halves(h)
        for i, (m, k) in enumerate(members):
            rows = slice(i * blocks, (i + 1) * blocks)
            to = slice(v * blocks, (v + 1) * blocks)
            right[g * len(members) + i, to, :LANES] = high[rows, :]
            right[g * len(members) + i, to, LANES:] = low[rows, :]

    def keep_second(g, v, h):
        f[pl.ds(v * half_rows + g * span, span), :] = h

    def spread_views(g):
        for v in range(views):
            lhs = stacked(turned(0, g, v) + turned(1, g, v))
            h = jnp.dot(lhs, resp_t[v], preferred_element_type=jnp.float32)
            keep_first(g, v, h[:span, :])
            keep_second(g, v, h[span:, :])

    def mix_first(g):
        for i in range(len(members)):
            t = g * len(members) + i
            both = jnp.dot(couple[t, 0], right[t], preferred_element_type=jnp.float32)
            both = both + jnp.dot(couple[t, 1], right[t], preferred_element_type=jnp.float32)
            mixed = both[:, :LANES] + both[:, LANES:]
            high, low = halves(mixed)
            for w in range(views):
                rows = slice(w * blocks, (w + 1) * blocks)
                zs[w, i * blocks : (i + 1) * blocks, :LANES] = high[rows, :]
                zs[w, i * blocks : (i + 1) * blocks, LANES:] = low[rows, :]

    def mix_second(g, w, slot):
        for i, (m, k) in enumerate(members):
            total = None
            for v in range(views):
                here = f[pl.ds(g * span + v * half_rows + i * blocks, blocks), :]
                row = (g * group + m) * per_device + v * tiles + k
                row = (2 * row + w // half_views) * table_rows + w % half_views
                factor = coef[pl.ds(row, 8, stride=0), :]
                term = jnp.concatenate([factor] * (blocks // 8), axis=0) * here
                total = term if total is None else total + term
            high, low = halves(total)
            rows = slice(i * blocks, (i + 1) * blocks)
            slot[rows, :LANES] = high
            slot[rows, LANES:] = low

    def gather(n, g, w, slot, hd):
        h = jnp.dot(slot[...], resp[w], preferred_element_type=jnp.float32)
        for i in range(len(members)):
            part = h[i * blocks : (i + 1) * blocks, :]
            hd[2 * i * blocks : (2 * i + 1) * blocks, :] = part
            hd[(2 * i + 1) * blocks : (2 * i + 2) * blocks, :] = part
        total = gy[w * blocks : (w + 1) * blocks, :]
        for i, (m, k) in enumerate(members):
            device = n * half + g * group + m
            total = total + turn(hd, 2 * i * blocks, device, w * tiles + k, -1)
        gy[w * blocks : (w + 1) * blocks, :] = total

    def mix_and_gather(g):
        mix_first(g)
        for w in range(views):
            mix_second(g, w, z2.at[w % 4])
            gather(1, g, w, z2.at[w % 4], hds[w % 2])
            gather(0, g, w, zs.at[w], hds[2 + w % 2])

    def apply():
        gy[...] = jnp.zeros_like(gy)
        if groups == 1:
            spread_views(0)
            mix_and_gather(0)
        else:
            lax.fori_loop(0, groups, lambda g, carry: (spread_views(g), carry)[1], 0)
            lax.fori_loop(0, groups, lambda g, carry: (mix_and_gather(g), carry)[1], 0)

    start = meas[...] - (first[:size, :] + second[:size, :])
    y[...] = start
    double(start)
    zero = jnp.zeros_like(start)
    d[...] = zero
    gd[...] = zero
    step[...] = zero
    for t in range(half * tiles):
        right[t, size:, :] = jnp.zeros((2 * LANES - size, 2 * LANES), jnp.bfloat16)

    def broadcast_one(device, carry):
        here = second[pl.ds(pl.multiple_of(size + device * table_rows, 8), table_rows), :]
        for c in range(per_device):
            for side in range(2):
                rows = pl.multiple_of((2 * (device * per_device + c) + side) * table_rows, 8)
                lane_of = side * (LANES // 2) + c
                coef[pl.ds(rows, table_rows), :] = jnp.broadcast_to(
                    here[:, lane_of : lane_of + 1], here.shape
                )
        return carry

    lax.fori_loop(0, half, broadcast_one, 0)
    to_scalars.wait()

    def iterate(n, norm_before):
        apply()
        new_y, new_gy = y[...], gy[...]
        norm = jnp.sum(new_y * new_gy)
        beta = jnp.where(n == 0, 0.0, norm / norm_before)
        new_d = new_y + beta * d[...]
        new_gd = new_gy + beta * gd[...]
        product = jnp.sum(new_gd * new_gd) + jnp.sum(new_d * new_gd) / TAU_STEP
        alpha = norm / product
        d[...] = new_d
        gd[...] = new_gd
        step[...] = step[...] + alpha * new_d
        new_y = new_y - alpha * (new_gd + new_d / TAU_STEP)
        y[...] = new_y
        double(new_y)
        return norm

    lax.fori_loop(0, CG_ITERS, iterate, jnp.float32(1.0))

    double(step[...])
    own = tiles * blocks
    for v in range(views):
        lhs = stacked(
            [
                pull(
                    lambda q: wd[pl.ds(2 * v * blocks + q, blocks), :],
                    bins[k, angles[0, v]], lane,
                )
                for k in range(tiles)
            ]
        )
        fs[v * own : (v + 1) * own, :] = jnp.dot(
            lhs, resp_t[v], preferred_element_type=jnp.float32
        )
    for b in range(0, blocks, 2):
        picked = [fs[pl.ds(b + n, views * tiles, stride=blocks), :] for n in range(2)]
        here = slice(b * LANES, (b + 2) * LANES)
        out[:, here] = (
            image[:, here]
            - TAU_STEP * (behind[:, here] - dual_new[:, here])
            + product(spread[...], jnp.concatenate(picked, axis=1))
        )


VMEM = pl.BlockSpec(memory_space=pltpu.VMEM)
SMEM = pl.BlockSpec(memory_space=pltpu.SMEM)
PLACE = pl.BlockSpec(memory_space=pl.ANY)


def f32(*shape):
    return pltpu.VMEM(shape, jnp.float32)


def stay(x):
    return pltpu.with_memory_space_constraint(x, pltpu.MemorySpace.HBM)


def kernel(body, out_shape, scalars, arrays, scratch=(), limit=16 << 20, in_place=()):
    single = not isinstance(out_shape, tuple)
    return pl.pallas_call(
        body,
        out_shape=out_shape,
        in_specs=[SMEM] * len(scalars) + [VMEM] * len(arrays) + [PLACE] * len(in_place),
        out_specs=VMEM if single else (VMEM,) * len(out_shape),
        scratch_shapes=list(scratch),
        compiler_params=pltpu.CompilerParams(vmem_limit_bytes=limit),
    )(
        *(stay(a) if lies else a for a, lies in scalars),
        *(pltpu.with_memory_space_constraint(a, pltpu.MemorySpace.VMEM) for a in arrays),
        *map(stay, in_place),
    )


def exchange(x, sizes, ahead, mask):
    phases, rows = sizes
    pairs = [
        (t * rows + r, ((t + ahead) % phases) * rows + (r ^ mask))
        for t in range(phases)
        for r in range(rows)
    ]
    return lax.ppermute(x, ("tm", "row"), pairs)


def local(image, relaxed, dual, sinogram, angle_index, bin_offset, row_weight, response, row_gain):
    phases, devices = lax.axis_size("tm"), lax.axis_size("row")
    sizes = (phases, devices)
    num_rows, cols = image.shape[2:]
    views = angle_index.shape[1]
    tiles = bin_offset.shape[0]
    blocks = cols // LANES
    size = views * blocks
    image2, relaxed2, dual2 = (a.reshape(num_rows, cols) for a in (image, relaxed, dual))

    ring = [(i, (i - 1) % phases) for i in range(phases)]
    next_angles = lax.ppermute(angle_index, "tm", ring)
    ahead = lax.ppermute(relaxed2, "tm", ring)

    gain = row_gain.reshape(1, num_rows)
    meas = sinogram.reshape(size, LANES)
    table_rows = -(-(views // 2 + 1) // 8) * 8
    assert views % 2 == 0 and tiles * views <= LANES // 2
    dims = dict(tiles=tiles, views=views, blocks=blocks)
    twice = pltpu.VMEM((views, 2 * LANES, LANES), jnp.bfloat16)
    spreads = f32(views * tiles, num_rows)
    tall = pltpu.VMEM((row_weight.shape[0], num_rows), jnp.float32)

    own_angles, offsets = (angle_index, True), (bin_offset, True)
    resp, resp_t, spread, spread_t, table, before, rest, gained = kernel(
        functools.partial(own_kernel, **dims),
        (
            twice, twice, spreads, f32(num_rows, views * tiles), f32(table_rows, LANES),
            f32(size, LANES), f32(num_rows, cols), tall,
        ),
        (own_angles, offsets),
        (),
        project_scratch(1, **dims)
        + [
            pltpu.VMEM((-(-views // 8) * 8, num_rows), jnp.float32),
            pltpu.VMEM(row_weight.shape[::-1], jnp.float32),
            pltpu.VMEM(gain.shape, jnp.float32),
            pltpu.VMEM((3, num_rows, cols), jnp.float32),
            pltpu.SemaphoreType.DMA((2 * views + 5,)),
        ],
        in_place=(row_weight.T, gain, image2, dual2, relaxed2, response),
    )
    resp_next, spread_next = kernel(
        functools.partial(next_kernel, tiles=tiles, views=views),
        (twice, spreads),
        ((next_angles, False),),
        (gained,),
        [pltpu.SemaphoreType.DMA((2 * views,))],
        in_place=(response,),
    )
    dual_new, msg, msg_next = kernel(
        functools.partial(dual_kernel, **dims),
        (f32(num_rows, cols), f32(size + table_rows, LANES), f32(size, LANES)),
        (own_angles, (next_angles, False), offsets),
        (rest, ahead, spread, spread_next, resp, resp_next, before, table),
        project_scratch(2, **dims),
    )

    masks = [1 << b if b < 2 else 3 << (b - 1) for b in range(devices.bit_length() - 1)]
    masks = masks[:1] + masks[:0:-1]
    got = exchange(msg, sizes, 0, masks[0])
    got_next = exchange(msg_next, sizes, 1, 0)
    got_cross = exchange(msg_next, sizes, 1, masks[0])
    total = msg[:size] + got[:size] + (got_next + got_cross)
    tables = jnp.concatenate([msg[size:], got[size:]], axis=0)
    for mask in masks[1:]:
        msg = jnp.concatenate([total, tables], axis=0)
        got = exchange(msg, sizes, 0, mask)
        total = msg[:size] + got[:size]
        tables = jnp.concatenate([msg[size:], got[size:]], axis=0)
    half = devices // 2
    couple = kernel(
        functools.partial(couple_kernel, size=size, table_rows=table_rows, **dims),
        pltpu.VMEM((half * tiles, 2, size, 2 * LANES), jnp.bfloat16),
        (),
        (msg,),
        [pltpu.VMEM((4 * half * tiles * table_rows, 2 * LANES), jnp.float32)],
        limit=(4 << 20) + half * tiles * (4 * table_rows * 2 * LANES * 4),
    )
    behind = lax.ppermute(dual_new, "tm", [(i, (i + 1) % phases) for i in range(phases)])

    group = max(1, 16 // tiles)
    while half % group:
        group //= 2
    whole = half * tiles * blocks
    span = group * tiles * blocks
    image_new = kernel(
        functools.partial(
            cg_kernel, **dims, devices=devices, group=group, table_rows=table_rows
        ),
        jax.ShapeDtypeStruct((num_rows, cols), jnp.float32),
        (own_angles, offsets),
        (couple, msg, got, meas, resp, resp_t, spread_t, image2, dual_new, behind),
        [pltpu.VMEM((size, LANES), jnp.float32)] * 5
        + [
            pltpu.VMEM((2 * size, LANES), jnp.float32),
            pltpu.VMEM((views * whole, LANES), jnp.float32),
            pltpu.VMEM((half * tiles, 2 * LANES, 2 * LANES), jnp.bfloat16),
            pltpu.VMEM((4, span, 2 * LANES), jnp.bfloat16),
            pltpu.VMEM((views, span, 2 * LANES), jnp.bfloat16),
        ]
        + [pltpu.VMEM((2 * span, LANES), jnp.float32)] * 4
        + [
            pltpu.VMEM((views * tiles * blocks, LANES), jnp.float32),
            pltpu.VMEM((2 * half * tiles * views * table_rows, LANES), jnp.float32),
            pltpu.VMEM((4 * devices, LANES), jnp.int32),
            pltpu.SMEM((4 * devices, LANES), jnp.int32),
            pltpu.SemaphoreType.DMA,
        ],
        limit=(12 << 20) + 14 * views * whole * LANES,
    )
    return image_new.reshape(image.shape), dual_new.reshape(dual.shape)


def solution(mesh):
    return jax.shard_map(
        local,
        mesh=mesh,
        in_specs=(
            P("tm", None, "row", None),
            P("tm", None, "row", None),
            P("tm", None, "row", None),
            P("tm", None, None, None),
            P("tm", None),
            P("row", None),
            P(),
            P(),
            P("row"),
        ),
        out_specs=(P("tm", None, "row", None), P("tm", None, "row", None)),
        check_vma=False,
    )
```

profile of v0, /device:TPU:0, one launch (start us, length us, event | category | flops | bytes accessed | tf_op | source)
XLA Modules:
  0.0 49.7 jit_solution(8897412770430136680)
XLA Ops:
  0.6 2.5 %collective-permute-start.1 = (f32[64,2048]{1,0:T(8,128)}, f32[64,2048]{1,0:T(8,128)S(1)}, u32[]{:S(2)}, u32[]{:S(2)}) collective-permute-start(f32[64,2048]{1,0:T(8,128)} %bitcast.13), channel_id=1, source_target_pairs={{0,24},{8,0},{16,8},{24,16},{1,25},{9,1},{17,9},{25,17},{2,26},{10... | collective-permute-start | bytes 1572872 | tf_op jit(solution)/shard_map/ppermute | solution.py:455
  3.1 0.7 %collective-permute-start = (s32[1,12]{1,0:T(1,128)}, s32[1,12]{1,0:T(1,128)S(1)}, u32[]{:S(2)}, u32[]{:S(2)}) collective-permute-start(s32[1,12]{1,0:T(1,128)} %angles.5), channel_id=1, source_target_pairs={{0,24},{8,0},{16,8},{24,16},{1,25},{9,1},{17,9},{25,17},{2,26},{10... | collective-permute-start | bytes 152 | tf_op jit(solution)/shard_map/ppermute | solution.py:454
  3.8 3.8 %shard_map.104 = (bf16[12,256,128]{2,1,0:T(8,128)(2,1)S(1)}, bf16[12,256,128]{2,1,0:T(8,128)(2,1)S(1)}, f32[48,64]{1,0:T(8,128)S(1)}, f32[64,48]{1,0:T(8,128)S(1...) custom-call(s32[1,12]{1,0:T(1,128)} %angles.5, ...), custom_call_target="tpu_custom_call" | custom-call | tf_op jit(solution)/shard_map/pallas_call | solution.py:419
  7.6 2.5 %collective-permute-done.angles.angles_next = s32[1,12]{1,0:T(1,128)S(1)} collective-permute-done((s32[1,12]{1,0:T(1,128)}, s32[1,12]{1,0:T(1,128)S(1)}, u32[]{:S(2)}, u32[]{:S(2)}) %collective-permute-start) | collective-permute-done | bytes 80 | tf_op jit(solution)/shard_map/ppermute | solution.py:454
  10.1 1.9 %shard_map.105 = (bf16[12,256,128]{2,1,0:T(8,128)(2,1)S(1)}, f32[48,64]{1,0:T(8,128)S(1)}) custom-call(s32[1,12]{1,0:T(1,128)S(1)} %collective-permute-done.angles.angles_next, f32[32,64]{1,0:T(8,128)S(1)} %get-tuple-element.17.gained, bf16[32,128,128]{2,1,0:T(8,128)(2,1)} %response.3), custom_call_target="tpu_custom_call" | custom-call | tf_op jit(solution)/shard_map/pallas_call | solution.py:419
  12.0 0.0 collective-permute-done.1.ahead
  12.0 1.9 %shard_map.106 = (f32[64,2048]{1,0:T(8,128)S(1)}, f32[200,128]{1,0:T(8,128)S(1)}, f32[192,128]{1,0:T(8,128)S(1)}) custom-call(s32[1,12]{1,0:T(1,128)} %angles.5, s32[1,12]{1,0:T(1,128)S(1)} %collective-permute-done.angles.angles_next, s32[4,32]{1,0:T(4,128)} %bins.5, f32[64,2048]{1,0:T(8,128)S(1)} %get-tuple-element.15.rest, ...), custom_call_target="tpu_custom_call" | custom-call | tf_op jit(solution)/shard_map/pallas_call | solution.py:419
  13.9 0.0 copy-start
  13.9 0.0 copy-start.1
  13.9 1.6 %collective-permute-start.2 = (f32[200,128]{1,0:T(8,128)S(1)}, f32[200,128]{1,0:T(8,128)S(1)}, u32[]{:S(2)}, u32[]{:S(2)}) collective-permute-start(f32[200,128]{1,0:T(8,128)S(1)} %get-tuple-element.23), channel_id=1, source_target_pairs={{0,1},{1,0},{2,3},{3,2},{4,5},{5,4},{6,7},{7,6},{8,9},{9,8},{10,11... | collective-permute-start | bytes 307208 | tf_op jit(solution)/shard_map/ppermute | solution.py:440
  15.5 0.5 %collective-permute-start.3 = (f32[192,128]{1,0:T(8,128)S(1)}, f32[192,128]{1,0:T(8,128)S(1)}, u32[]{:S(2)}, u32[]{:S(2)}) collective-permute-start(f32[192,128]{1,0:T(8,128)S(1)} %get-tuple-element.24), channel_id=1, source_target_pairs={{0,8},{1,9},{2,10},{3,11},{4,12},{5,13},{6,14},{7,15},{8,16},{9,17... | collective-permute-start | bytes 294920 | tf_op jit(solution)/shard_map/ppermute | solution.py:440
  16.0 0.3 collective-permute-start.4
  16.3 3.3 %collective-permute-done.2 = f32[200,128]{1,0:T(8,128)S(1)} collective-permute-done((f32[200,128]{1,0:T(8,128)S(1)}, f32[200,128]{1,0:T(8,128)S(1)}, u32[]{:S(2)}, u32[]{:S(2)}) %collective-permute-start.2) | collective-permute-done | bytes 102432 | tf_op jit(solution)/shard_map/ppermute | solution.py:440
  19.6 0.0 collective-permute-done.3
  19.6 1.5 %collective-permute-done.4 = f32[192,128]{1,0:T(8,128)S(1)} collective-permute-done((f32[192,128]{1,0:T(8,128)S(1)}, f32[192,128]{1,0:T(8,128)S(1)}, u32[]{:S(2)}, u32[]{:S(2)}) %collective-permute-start.4) | collective-permute-done | bytes 98336 | tf_op jit(solution)/shard_map/ppermute | solution.py:440
  21.1 3.7 %collective-permute-start.5 = (f32[208,128]{1,0:T(8,128)S(1)}, f32[208,128]{1,0:T(8,128)S(1)}, u32[]{:S(2)}, u32[]{:S(2)}) collective-permute-start(f32[208,128]{1,0:T(8,128)S(1)} %pad_maximum_fusion.1), channel_id=1, source_target_pairs={{0,6},{1,7},{2,4},{3,5},{4,2},{5,3},{6,0},{7,1},{8,14},{9,15},{10,... | collective-permute-start | bytes 319496 | tf_op jit(solution)/shard_map/ppermute | solution.py:440
  24.8 0.1 collective-permute-start.7
  24.9 3.5 %collective-permute-done.5 = f32[208,128]{1,0:T(8,128)S(1)} collective-permute-done((f32[208,128]{1,0:T(8,128)S(1)}, f32[208,128]{1,0:T(8,128)S(1)}, u32[]{:S(2)}, u32[]{:S(2)}) %collective-permute-start.5) | collective-permute-done | bytes 106528 | tf_op jit(solution)/shard_map/ppermute | solution.py:440
  28.5 2.0 %collective-permute-start.6 = (f32[224,128]{1,0:T(8,128)S(1)}, f32[224,128]{1,0:T(8,128)S(1)}, u32[]{:S(2)}, u32[]{:S(2)}) collective-permute-start(f32[224,128]{1,0:T(8,128)S(1)} %pad_maximum_fusion.first), channel_id=1, source_target_pairs={{0,2},{1,3},{2,0},{3,1},{4,6},{5,7},{6,4},{7,5},{8,10},{9,11},{10,... | collective-permute-start | bytes 344072 | tf_op jit(solution)/shard_map/ppermute | solution.py:440
  30.4 0.8 %copy.11 = f32[1,1,64,2048]{3,2,1,0:T(8,128)} copy(f32[1,1,64,2048]{3,2,1,0:T(8,128)S(1)} %bitcast.8) | data formatting | bytes 1048576
  31.2 0.9 %shard_map.107.couple = bf16[16,2,192,256]{3,2,1,0:T(8,128)(2,1)S(1)} custom-call(f32[224,128]{1,0:T(8,128)S(1)} %pad_maximum_fusion.first), custom_call_target="tpu_custom_call" | custom-call | tf_op jit(solution)/shard_map/pallas_call | solution.py:419
  32.1 1.2 %collective-permute-done.6.second = f32[224,128]{1,0:T(8,128)S(1)} collective-permute-done((f32[224,128]{1,0:T(8,128)S(1)}, f32[224,128]{1,0:T(8,128)S(1)}, u32[]{:S(2)}, u32[]{:S(2)}) %collective-permute-start.6) | collective-permute-done | bytes 114720 | tf_op jit(solution)/shard_map/ppermute | solution.py:440
  33.3 0.1 collective-permute-done.7.behind
  33.4 0.0 copy-done
  33.4 0.0 copy-done.1
  33.4 16.4 %shard_map.108 = f32[64,2048]{1,0:T(8,128)} custom-call(s32[1,12]{1,0:T(1,128)} %angles.5, s32[4,32]{1,0:T(4,128)} %bins.5, bf16[16,2,192,256]{3,2,1,0:T(8,128)(2,1)S(1)} %shard_map.107.couple, f32[224,128]{1,0:T(8,128)S(1)} %pad_maximum_fusion.first, f32[224,128]{1,0:T(8,128)S(1)} %collective-permute-done.6.second, f32[192,128]{1,0:T(8,128)S(1)} %bitcast.11, ...), custom_call_target="tpu_custom_call" | custom-call | tf_op jit(solution)/shard_map/pallas_call | solution.py:419
  (7 shorter events, 0.1 us)
Async XLA Ops:
  0.6 11.4 %collective-permute-start.1 = (f32[64,2048]{1,0:T(8,128)}, f32[64,2048]{1,0:T(8,128)S(1)}, u32[]{:S(2)}, u32[]{:S(2)}) collective-permute-start(f32[64,2048]{1,0:T(8,128)} %bitcast.13), channel_id=1, source_target_pairs={{0,24},{8,0},{16,8},{24,16},{1,25},{9,1},{17,9},{25,17},{2,26},{10... | collective-permute-start | bytes 1572872 | tf_op jit(solution)/shard_map/ppermute | solution.py:455
  3.1 7.0 %collective-permute-start = (s32[1,12]{1,0:T(1,128)}, s32[1,12]{1,0:T(1,128)S(1)}, u32[]{:S(2)}, u32[]{:S(2)}) collective-permute-start(s32[1,12]{1,0:T(1,128)} %angles.5), channel_id=1, source_target_pairs={{0,24},{8,0},{16,8},{24,16},{1,25},{9,1},{17,9},{25,17},{2,26},{10... | collective-permute-start | bytes 152 | tf_op jit(solution)/shard_map/ppermute | solution.py:454
  13.9 19.5 %copy-start = (f32[1,1,64,2048]{3,2,1,0:T(8,128)S(1)}, f32[1,1,64,2048]{3,2,1,0:T(8,128)}, u32[]{:S(2)}) copy-start(f32[1,1,64,2048]{3,2,1,0:T(8,128)} %param.9) | copy-start | bytes 1572868
  13.9 19.5 %copy-start.1 = (f32[1,12,1,2048]{3,2,1,0:T(1,128)S(1)}, f32[1,12,1,2048]{3,2,1,0:T(1,128)}, u32[]{:S(2)}) copy-start(f32[1,12,1,2048]{3,2,1,0:T(1,128)} %param.12) | copy-start | bytes 294916
  13.9 5.7 %collective-permute-start.2 = (f32[200,128]{1,0:T(8,128)S(1)}, f32[200,128]{1,0:T(8,128)S(1)}, u32[]{:S(2)}, u32[]{:S(2)}) collective-permute-start(f32[200,128]{1,0:T(8,128)S(1)} %get-tuple-element.23), channel_id=1, source_target_pairs={{0,1},{1,0},{2,3},{3,2},{4,5},{5,4},{6,7},{7,6},{8,9},{9,8},{10,11... | collective-permute-start | bytes 307208 | tf_op jit(solution)/shard_map/ppermute | solution.py:440
  15.5 4.1 %collective-permute-start.3 = (f32[192,128]{1,0:T(8,128)S(1)}, f32[192,128]{1,0:T(8,128)S(1)}, u32[]{:S(2)}, u32[]{:S(2)}) collective-permute-start(f32[192,128]{1,0:T(8,128)S(1)} %get-tuple-element.24), channel_id=1, source_target_pairs={{0,8},{1,9},{2,10},{3,11},{4,12},{5,13},{6,14},{7,15},{8,16},{9,17... | collective-permute-start | bytes 294920 | tf_op jit(solution)/shard_map/ppermute | solution.py:440
  16.0 5.0 %collective-permute-start.4 = (f32[192,128]{1,0:T(8,128)S(1)}, f32[192,128]{1,0:T(8,128)S(1)}, u32[]{:S(2)}, u32[]{:S(2)}) collective-permute-start(f32[192,128]{1,0:T(8,128)S(1)} %get-tuple-element.24), channel_id=1, source_target_pairs={{0,9},{1,8},{2,11},{3,10},{4,13},{5,12},{6,15},{7,14},{8,17},{9,16... | collective-permute-start | bytes 294920 | tf_op jit(solution)/shard_map/ppermute | solution.py:440
  21.1 7.3 %collective-permute-start.5 = (f32[208,128]{1,0:T(8,128)S(1)}, f32[208,128]{1,0:T(8,128)S(1)}, u32[]{:S(2)}, u32[]{:S(2)}) collective-permute-start(f32[208,128]{1,0:T(8,128)S(1)} %pad_maximum_fusion.1), channel_id=1, source_target_pairs={{0,6},{1,7},{2,4},{3,5},{4,2},{5,3},{6,0},{7,1},{8,14},{9,15},{10,... | collective-permute-start | bytes 319496 | tf_op jit(solution)/shard_map/ppermute | solution.py:440
  24.8 8.6 %collective-permute-start.7 = (f32[64,2048]{1,0:T(8,128)S(1)}, f32[64,2048]{1,0:T(8,128)S(1)}, u32[]{:S(2)}, u32[]{:S(2)}) collective-permute-start(f32[64,2048]{1,0:T(8,128)S(1)} %get-tuple-element.27.dual_new), channel_id=1, source_target_pairs={{0,8},{8,16},{16,24},{24,0},{1,9},{9,17},{17,25},{25,1},{2,10},{10... | collective-permute-start | bytes 1572872 | tf_op jit(solution)/shard_map/ppermute | solution.py:522
  28.5 4.9 %collective-permute-start.6 = (f32[224,128]{1,0:T(8,128)S(1)}, f32[224,128]{1,0:T(8,128)S(1)}, u32[]{:S(2)}, u32[]{:S(2)}) collective-permute-start(f32[224,128]{1,0:T(8,128)S(1)} %pad_maximum_fusion.first), channel_id=1, source_target_pairs={{0,2},{1,3},{2,0},{3,1},{4,6},{5,7},{6,4},{7,5},{8,10},{9,11},{10,... | collective-permute-start | bytes 344072 | tf_op jit(solution)/shard_map/ppermute | solution.py:440
where the time goes:
time: 50.1 us; the launch traced here: 49.7 us
  Pallas kernels  24.9 us (50%)
  waiting for transfers between devices  12 us (24%)
  starting transfers between devices  11.3 us (23%)
  local copies, waits for them, and re-layouts  0.81 us (2%)
  between operations  0.71 us (1%)
    pallas_call x5, Pallas kernels, kernel(): pl.pallas_call(body, out_shape=out_shape, in_specs=[SMEM] * len(scalars)...  24.9 us
    ppermute x5, waiting for transfers between devices, exchange(): return lax.ppermute(x, ('tm', 'row'), pairs)  9.47 us
    ppermute x5, starting transfers between devices, exchange(): return lax.ppermute(x, ('tm', 'row'), pairs)  8 us
    ppermute x1, waiting for transfers between devices, local(): next_angles = lax.ppermute(angle_index, 'tm', ring)  2.48 us
    ppermute x1, starting transfers between devices, local(): ahead = lax.ppermute(relaxed2, 'tm', ring)  2.46 us
  transfers between devices with their start and end apart: 8, of which 6 were waited for; matrix products, arithmetic and copies ran while one was open for 2% of the time, Pallas kernels for 13%

commit v1 on v0

--- a/solution.py
+++ b/solution.py
@@ -24,8 +24,10 @@
 
 def product(a, b):
     (ah, al), (bh, bl) = halves(a), halves(b)
+    rows = a.shape[0]
     dot = functools.partial(jnp.dot, preferred_element_type=jnp.float32)
-    return dot(ah, bh) + (dot(ah, bl) + dot(al, bh))
+    both = dot(jnp.concatenate([ah, al], axis=0), bh)
+    return both[:rows] + (both[rows:] + dot(ah, bl))
 
 
 def lane_index(rows):
@@ -281,8 +283,12 @@
     def mix_first(g):
         for i in range(len(members)):
             t = g * len(members) + i
-            both = jnp.dot(couple[t, 0], right[t], preferred_element_type=jnp.float32)
-            both = both + jnp.dot(couple[t, 1], right[t], preferred_element_type=jnp.float32)
+            both = jnp.dot(
+                couple[t, 0, :, :size], right[t, :size, :], preferred_element_type=jnp.float32
+            )
+            both = both + jnp.dot(
+                couple[t, 1, :, :size], right[t, :size, :], preferred_element_type=jnp.float32
+            )
             mixed = both[:, :LANES] + both[:, LANES:]
             high, low = halves(mixed)
             for w in range(views):

time: 50.1 us -> 50 us (level)
  transfers between devices with their start and end apart: 8 -> 8, of which waited for: 6 -> 5; matrix products, arithmetic and copies ran while one was open for 2% -> 2% of each run, Pallas kernels for 13% -> 13%
where the time goes in v1:
time: 50 us; the launch traced here: 49.7 us
  Pallas kernels  24.7 us (49%)
  waiting for transfers between devices  12.1 us (24%)
  starting transfers between devices  11.3 us (23%)
  local copies, waits for them, and re-layouts  0.81 us (2%)
  between operations  0.71 us (1%)
    pallas_call x5, Pallas kernels, kernel(): pl.pallas_call(body, out_shape=out_shape, in_specs=[SMEM] * len(scalars)...  24.7 us
    ppermute x5, waiting for transfers between devices, exchange(): return lax.ppermute(x, ('tm', 'row'), pairs)  9.47 us
    ppermute x5, starting transfers between devices, exchange(): return lax.ppermute(x, ('tm', 'row'), pairs)  7.99 us
    ppermute x1, waiting for transfers between devices, local(): next_angles = lax.ppermute(angle_index, 'tm', ring)  2.56 us
    ppermute x1, starting transfers between devices, local(): ahead = lax.ppermute(relaxed2, 'tm', ring)  2.46 us
  transfers between devices with their start and end apart: 8, of which 5 were waited for; matrix products, arithmetic and copies ran while one was open for 2% of the time, Pallas kernels for 13%

profile of v1, /device:TPU:0, one launch (start us, length us, event | category | flops | bytes accessed | tf_op | source)
XLA Modules:
  0.0 49.7 jit_solution(6086577366100351791)
XLA Ops:
  0.6 2.5 %collective-permute-start.1 = (f32[64,2048]{1,0:T(8,128)}, f32[64,2048]{1,0:T(8,128)S(1)}, u32[]{:S(2)}, u32[]{:S(2)}) collective-permute-start(f32[64,2048]{1,0:T(8,128)} %bitcast.13), channel_id=1, source_target_pairs={{0,24},{8,0},{16,8},{24,16},{1,25},{9,1},{17,9},{25,17},{2,26},{10... | collective-permute-start | bytes 1572872 | tf_op jit(solution)/shard_map/ppermute | solution.py:461
  3.1 0.7 %collective-permute-start = (s32[1,12]{1,0:T(1,128)}, s32[1,12]{1,0:T(1,128)S(1)}, u32[]{:S(2)}, u32[]{:S(2)}) collective-permute-start(s32[1,12]{1,0:T(1,128)} %angles.5), channel_id=1, source_target_pairs={{0,24},{8,0},{16,8},{24,16},{1,25},{9,1},{17,9},{25,17},{2,26},{10... | collective-permute-start | bytes 152 | tf_op jit(solution)/shard_map/ppermute | solution.py:460
  3.8 3.8 %shard_map.104 = (bf16[12,256,128]{2,1,0:T(8,128)(2,1)S(1)}, bf16[12,256,128]{2,1,0:T(8,128)(2,1)S(1)}, f32[48,64]{1,0:T(8,128)S(1)}, f32[64,48]{1,0:T(8,128)S(1...) custom-call(s32[1,12]{1,0:T(1,128)} %angles.5, ...), custom_call_target="tpu_custom_call" | custom-call | tf_op jit(solution)/shard_map/pallas_call | solution.py:425
  7.5 2.6 %collective-permute-done.angles.angles_next = s32[1,12]{1,0:T(1,128)S(1)} collective-permute-done((s32[1,12]{1,0:T(1,128)}, s32[1,12]{1,0:T(1,128)S(1)}, u32[]{:S(2)}, u32[]{:S(2)}) %collective-permute-start) | collective-permute-done | bytes 80 | tf_op jit(solution)/shard_map/ppermute | solution.py:460
  10.1 1.9 %shard_map.105 = (bf16[12,256,128]{2,1,0:T(8,128)(2,1)S(1)}, f32[48,64]{1,0:T(8,128)S(1)}) custom-call(s32[1,12]{1,0:T(1,128)S(1)} %collective-permute-done.angles.angles_next, f32[32,64]{1,0:T(8,128)S(1)} %get-tuple-element.17.gained, bf16[32,128,128]{2,1,0:T(8,128)(2,1)} %response.3), custom_call_target="tpu_custom_call" | custom-call | tf_op jit(solution)/shard_map/pallas_call | solution.py:425
  12.0 0.0 collective-permute-done.1.ahead
  12.0 1.9 %shard_map.106 = (f32[64,2048]{1,0:T(8,128)S(1)}, f32[200,128]{1,0:T(8,128)S(1)}, f32[192,128]{1,0:T(8,128)S(1)}) custom-call(s32[1,12]{1,0:T(1,128)} %angles.5, s32[1,12]{1,0:T(1,128)S(1)} %collective-permute-done.angles.angles_next, s32[4,32]{1,0:T(4,128)} %bins.5, f32[64,2048]{1,0:T(8,128)S(1)} %get-tuple-element.15.rest, ...), custom_call_target="tpu_custom_call" | custom-call | tf_op jit(solution)/shard_map/pallas_call | solution.py:425
  13.9 0.0 copy-start
  13.9 0.0 copy-start.1
  13.9 1.6 %collective-permute-start.2 = (f32[200,128]{1,0:T(8,128)S(1)}, f32[200,128]{1,0:T(8,128)S(1)}, u32[]{:S(2)}, u32[]{:S(2)}) collective-permute-start(f32[200,128]{1,0:T(8,128)S(1)} %get-tuple-element.23), channel_id=1, source_target_pairs={{0,1},{1,0},{2,3},{3,2},{4,5},{5,4},{6,7},{7,6},{8,9},{9,8},{10,11... | collective-permute-start | bytes 307208 | tf_op jit(solution)/shard_map/ppermute | solution.py:446
  15.5 0.5 %collective-permute-start.3 = (f32[192,128]{1,0:T(8,128)S(1)}, f32[192,128]{1,0:T(8,128)S(1)}, u32[]{:S(2)}, u32[]{:S(2)}) collective-permute-start(f32[192,128]{1,0:T(8,128)S(1)} %get-tuple-element.24), channel_id=1, source_target_pairs={{0,8},{1,9},{2,10},{3,11},{4,12},{5,13},{6,14},{7,15},{8,16},{9,17... | collective-permute-start | bytes 294920 | tf_op jit(solution)/shard_map/ppermute | solution.py:446
  16.0 0.3 collective-permute-start.4
  16.3 3.3 %collective-permute-done.2 = f32[200,128]{1,0:T(8,128)S(1)} collective-permute-done((f32[200,128]{1,0:T(8,128)S(1)}, f32[200,128]{1,0:T(8,128)S(1)}, u32[]{:S(2)}, u32[]{:S(2)}) %collective-permute-start.2) | collective-permute-done | bytes 102432 | tf_op jit(solution)/shard_map/ppermute | solution.py:446
  19.6 0.0 collective-permute-done.3
  19.6 1.5 %collective-permute-done.4 = f32[192,128]{1,0:T(8,128)S(1)} collective-permute-done((f32[192,128]{1,0:T(8,128)S(1)}, f32[192,128]{1,0:T(8,128)S(1)}, u32[]{:S(2)}, u32[]{:S(2)}) %collective-permute-start.4) | collective-permute-done | bytes 98336 | tf_op jit(solution)/shard_map/ppermute | solution.py:446
  21.1 3.7 %collective-permute-start.5 = (f32[208,128]{1,0:T(8,128)S(1)}, f32[208,128]{1,0:T(8,128)S(1)}, u32[]{:S(2)}, u32[]{:S(2)}) collective-permute-start(f32[208,128]{1,0:T(8,128)S(1)} %pad_maximum_fusion.1), channel_id=1, source_target_pairs={{0,6},{1,7},{2,4},{3,5},{4,2},{5,3},{6,0},{7,1},{8,14},{9,15},{10,... | collective-permute-start | bytes 319496 | tf_op jit(solution)/shard_map/ppermute | solution.py:446
  24.8 0.1 collective-permute-start.7
  24.9 3.5 %collective-permute-done.5 = f32[208,128]{1,0:T(8,128)S(1)} collective-permute-done((f32[208,128]{1,0:T(8,128)S(1)}, f32[208,128]{1,0:T(8,128)S(1)}, u32[]{:S(2)}, u32[]{:S(2)}) %collective-permute-start.5) | collective-permute-done | bytes 106528 | tf_op jit(solution)/shard_map/ppermute | solution.py:446
  28.5 2.0 %collective-permute-start.6 = (f32[224,128]{1,0:T(8,128)S(1)}, f32[224,128]{1,0:T(8,128)S(1)}, u32[]{:S(2)}, u32[]{:S(2)}) collective-permute-start(f32[224,128]{1,0:T(8,128)S(1)} %pad_maximum_fusion.first), channel_id=1, source_target_pairs={{0,2},{1,3},{2,0},{3,1},{4,6},{5,7},{6,4},{7,5},{8,10},{9,11},{10,... | collective-permute-start | bytes 344072 | tf_op jit(solution)/shard_map/ppermute | solution.py:446
  30.4 0.8 %copy.11 = f32[1,1,64,2048]{3,2,1,0:T(8,128)} copy(f32[1,1,64,2048]{3,2,1,0:T(8,128)S(1)} %bitcast.8) | data formatting | bytes 1048576
  31.2 0.9 %shard_map.107.couple = bf16[16,2,192,256]{3,2,1,0:T(8,128)(2,1)S(1)} custom-call(f32[224,128]{1,0:T(8,128)S(1)} %pad_maximum_fusion.first), custom_call_target="tpu_custom_call" | custom-call | tf_op jit(solution)/shard_map/pallas_call | solution.py:425
  32.1 1.2 %collective-permute-done.6.second = f32[224,128]{1,0:T(8,128)S(1)} collective-permute-done((f32[224,128]{1,0:T(8,128)S(1)}, f32[224,128]{1,0:T(8,128)S(1)}, u32[]{:S(2)}, u32[]{:S(2)}) %collective-permute-start.6) | collective-permute-done | bytes 114720 | tf_op jit(solution)/shard_map/ppermute | solution.py:446
  33.3 0.1 collective-permute-done.7.behind
  33.4 0.0 copy-done
  33.4 0.0 copy-done.1
  33.4 16.3 %shard_map.108 = f32[64,2048]{1,0:T(8,128)} custom-call(s32[1,12]{1,0:T(1,128)} %angles.5, s32[4,32]{1,0:T(4,128)} %bins.5, bf16[16,2,192,256]{3,2,1,0:T(8,128)(2,1)S(1)} %shard_map.107.couple, f32[224,128]{1,0:T(8,128)S(1)} %pad_maximum_fusion.first, f32[224,128]{1,0:T(8,128)S(1)} %collective-permute-done.6.second, f32[192,128]{1,0:T(8,128)S(1)} %bitcast.11, ...), custom_call_target="tpu_custom_call" | custom-call | tf_op jit(solution)/shard_map/pallas_call | solution.py:425
  (7 shorter events, 0.1 us)
Async XLA Ops:
  0.6 11.4 %collective-permute-start.1 = (f32[64,2048]{1,0:T(8,128)}, f32[64,2048]{1,0:T(8,128)S(1)}, u32[]{:S(2)}, u32[]{:S(2)}) collective-permute-start(f32[64,2048]{1,0:T(8,128)} %bitcast.13), channel_id=1, source_target_pairs={{0,24},{8,0},{16,8},{24,16},{1,25},{9,1},{17,9},{25,17},{2,26},{10... | collective-permute-start | bytes 1572872 | tf_op jit(solution)/shard_map/ppermute | solution.py:461
  3.1 7.0 %collective-permute-start = (s32[1,12]{1,0:T(1,128)}, s32[1,12]{1,0:T(1,128)S(1)}, u32[]{:S(2)}, u32[]{:S(2)}) collective-permute-start(s32[1,12]{1,0:T(1,128)} %angles.5), channel_id=1, source_target_pairs={{0,24},{8,0},{16,8},{24,16},{1,25},{9,1},{17,9},{25,17},{2,26},{10... | collective-permute-start | bytes 152 | tf_op jit(solution)/shard_map/ppermute | solution.py:460
  13.9 19.5 %copy-start = (f32[1,1,64,2048]{3,2,1,0:T(8,128)S(1)}, f32[1,1,64,2048]{3,2,1,0:T(8,128)}, u32[]{:S(2)}) copy-start(f32[1,1,64,2048]{3,2,1,0:T(8,128)} %param.9) | copy-start | bytes 1572868
  13.9 19.5 %copy-start.1 = (f32[1,12,1,2048]{3,2,1,0:T(1,128)S(1)}, f32[1,12,1,2048]{3,2,1,0:T(1,128)}, u32[]{:S(2)}) copy-start(f32[1,12,1,2048]{3,2,1,0:T(1,128)} %param.12) | copy-start | bytes 294916
  13.9 5.7 %collective-permute-start.2 = (f32[200,128]{1,0:T(8,128)S(1)}, f32[200,128]{1,0:T(8,128)S(1)}, u32[]{:S(2)}, u32[]{:S(2)}) collective-permute-start(f32[200,128]{1,0:T(8,128)S(1)} %get-tuple-element.23), channel_id=1, source_target_pairs={{0,1},{1,0},{2,3},{3,2},{4,5},{5,4},{6,7},{7,6},{8,9},{9,8},{10,11... | collective-permute-start | bytes 307208 | tf_op jit(solution)/shard_map/ppermute | solution.py:446
  15.5 4.1 %collective-permute-start.3 = (f32[192,128]{1,0:T(8,128)S(1)}, f32[192,128]{1,0:T(8,128)S(1)}, u32[]{:S(2)}, u32[]{:S(2)}) collective-permute-start(f32[192,128]{1,0:T(8,128)S(1)} %get-tuple-element.24), channel_id=1, source_target_pairs={{0,8},{1,9},{2,10},{3,11},{4,12},{5,13},{6,14},{7,15},{8,16},{9,17... | collective-permute-start | bytes 294920 | tf_op jit(solution)/shard_map/ppermute | solution.py:446
  16.0 5.0 %collective-permute-start.4 = (f32[192,128]{1,0:T(8,128)S(1)}, f32[192,128]{1,0:T(8,128)S(1)}, u32[]{:S(2)}, u32[]{:S(2)}) collective-permute-start(f32[192,128]{1,0:T(8,128)S(1)} %get-tuple-element.24), channel_id=1, source_target_pairs={{0,9},{1,8},{2,11},{3,10},{4,13},{5,12},{6,15},{7,14},{8,17},{9,16... | collective-permute-start | bytes 294920 | tf_op jit(solution)/shard_map/ppermute | solution.py:446
  21.1 7.3 %collective-permute-start.5 = (f32[208,128]{1,0:T(8,128)S(1)}, f32[208,128]{1,0:T(8,128)S(1)}, u32[]{:S(2)}, u32[]{:S(2)}) collective-permute-start(f32[208,128]{1,0:T(8,128)S(1)} %pad_maximum_fusion.1), channel_id=1, source_target_pairs={{0,6},{1,7},{2,4},{3,5},{4,2},{5,3},{6,0},{7,1},{8,14},{9,15},{10,... | collective-permute-start | bytes 319496 | tf_op jit(solution)/shard_map/ppermute | solution.py:446
  24.8 8.6 %collective-permute-start.7 = (f32[64,2048]{1,0:T(8,128)S(1)}, f32[64,2048]{1,0:T(8,128)S(1)}, u32[]{:S(2)}, u32[]{:S(2)}) collective-permute-start(f32[64,2048]{1,0:T(8,128)S(1)} %get-tuple-element.27.dual_new), channel_id=1, source_target_pairs={{0,8},{8,16},{16,24},{24,0},{1,9},{9,17},{17,25},{25,1},{2,10},{10... | collective-permute-start | bytes 1572872 | tf_op jit(solution)/shard_map/ppermute | solution.py:528
  28.5 4.9 %collective-permute-start.6 = (f32[224,128]{1,0:T(8,128)S(1)}, f32[224,128]{1,0:T(8,128)S(1)}, u32[]{:S(2)}, u32[]{:S(2)}) collective-permute-start(f32[224,128]{1,0:T(8,128)S(1)} %pad_maximum_fusion.first), channel_id=1, source_target_pairs={{0,2},{1,3},{2,0},{3,1},{4,6},{5,7},{6,4},{7,5},{8,10},{9,11},{10,... | collective-permute-start | bytes 344072 | tf_op jit(solution)/shard_map/ppermute | solution.py:446
